TPU v7x, 256 devices: a whole 4x4x8 slice. The times are simulated.
256 devices in a mesh: grp: 8 (over y, core), sub: 32 (over x, z).
Axes of the slice: x: 4, y: 4, z: 8, core: 2. Of those that a mesh axis runs over, the one named last changes fastest.
Arguments:
- cluster_pos: float32 [3, 4096], P(None, 'sub'), may hold values from -3 to 3
- cluster_vel: float32 [3, 4096], P(None, 'sub'), may hold values from -15 to 15
- cluster_mass: float32 [4096], P('sub'), may hold values from 3 to 60
- galaxy_pos: float32 [3, 131072], P(None, ('grp', 'sub')), may hold values from -1 to 7
- galaxy_vel: float32 [3, 131072], P(None, ('grp', 'sub')), may hold values from -3 to 3
- galaxy_kind: int32 [131072], P(('grp', 'sub')), may hold values from 0 to 3
- species_mass: float32 [4], replicated, may hold values from 10 to 80
Outputs:
- cluster_pos_out: float32 [3, 4096], P(None, 'sub')
- cluster_vel_out: float32 [3, 4096], P(None, 'sub')
- galaxy_pos_out: float32 [3, 131072], P(None, ('grp', 'sub'))
- galaxy_vel_out: float32 [3, 131072], P(None, ('grp', 'sub'))
All inputs are finite; a program needn't handle non-finite values.
Results may differ from a plain program's by a relative error of at most 0.0003.
Values sent between devices are 32-bit elements; how exact they have to be, the bound alone decides.
A program may use at most 64 MiB of HBM per device.

v0:
```python
import jax
import jax.numpy as jnp
from jax import lax
from jax.sharding import PartitionSpec as P

SUBSTEPS = 8
step_time = 0.5
bridge_soft = 0.01
cluster_soft = 0.0025
tile_limit = 524288


def pick_block(target_count, source_count):
    tile_size = target_count
    while tile_size > 1 and (
        tile_size * source_count > tile_limit or target_count % tile_size != 0
    ):
        tile_size = tile_size // 2
    return tile_size


def field(targets, sources, masses, soften):
    target_count = targets.shape[1]
    tile_size = pick_block(target_count, sources.shape[1])

    def field_one_tile(target_tile):
        separation = sources[:, None, :] - target_tile[:, :, None]
        distance = jnp.sum(separation * separation, axis=0) + soften
        inverse = lax.rsqrt(distance)
        weight = masses[None, :] * inverse * inverse * inverse
        return jnp.sum(separation * weight[None], axis=2)

    stacked = targets.reshape(3, target_count // tile_size, tile_size).transpose(1, 0, 2)
    result = lax.map(field_one_tile, stacked)
    return result.transpose(1, 0, 2).reshape(3, target_count)


def rates(target_pos, target_vel, source_pos, source_vel, masses, soften):
    target_count = target_pos.shape[1]
    tile_size = pick_block(target_count, source_pos.shape[1])

    def rates_one_tile(target_tile):
        separation = source_pos[:, None, :] - target_tile[:3, :, None]
        closing = source_vel[:, None, :] - target_tile[3:, :, None]
        distance = jnp.sum(separation * separation, axis=0) + soften
        inverse = lax.rsqrt(distance)
        weight = masses[None, :] * inverse * inverse * inverse
        radial = 3.0 * jnp.sum(separation * closing, axis=0) / distance
        acceleration = jnp.sum(separation * weight[None], axis=2)
        jerk_rate = jnp.sum((closing - radial[None] * separation) * weight[None], axis=2)
        return jnp.concatenate([acceleration, jerk_rate], axis=0)

    stacked = jnp.concatenate([target_pos, target_vel], axis=0)
    stacked = stacked.reshape(6, target_count // tile_size, tile_size).transpose(1, 0, 2)
    result = lax.map(rates_one_tile, stacked)
    return result.transpose(1, 0, 2).reshape(6, target_count)


def local(
    cluster_pos, cluster_vel, cluster_mass, galaxy_pos, galaxy_vel, galaxy_kind, species_mass
):
    star_count = cluster_pos.shape[1]
    member_count = lax.axis_size("sub")
    group_count = lax.axis_size("grp")
    total_stars = star_count * member_count
    total_bodies = galaxy_pos.shape[1] * member_count * group_count
    star_mass = cluster_mass / total_stars
    species = jnp.arange(species_mass.shape[0], dtype=jnp.int32)
    body_mass = (
        jnp.sum(
            jnp.where(galaxy_kind[None, :] == species[:, None], species_mass[:, None], 0.0), axis=0
        )
        / total_bodies
    )
    half_step = step_time / 2.0

    def kick(star_positions, body_positions):
        stacked = jnp.concatenate([star_positions, star_mass[None, :]], axis=0)
        gathered = lax.all_gather(stacked, "sub", axis=1, tiled=True)
        galaxy_push = field(body_positions, gathered[:3], gathered[3], bridge_soft)
        partial_value = field(gathered[:3], body_positions, body_mass, bridge_soft)
        summed = lax.psum(partial_value, ("grp", "sub"))
        cluster_pull = lax.dynamic_slice_in_dim(
            summed, lax.axis_index("sub") * star_count, star_count, 1
        )
        return (cluster_pull, galaxy_push)

    def evaluate(guess_pos, guess_vel):
        sources = jnp.concatenate([guess_pos, guess_vel, star_mass[None, :]], axis=0)
        target_pos, target_vel = (guess_pos, guess_vel)
        source_piece = lax.all_gather(sources, "sub", axis=1, tiled=True)
        result = rates(
            target_pos,
            target_vel,
            source_piece[:3],
            source_piece[3:6],
            source_piece[6],
            cluster_soft,
        )
        return (result[:3], result[3:])

    first_pull, first_push = kick(cluster_pos, galaxy_pos)
    star_vel = cluster_vel + half_step * first_pull
    body_vel = galaxy_vel + half_step * first_push
    body_pos = galaxy_pos + step_time * body_vel
    substep_time = step_time / SUBSTEPS
    positions, velocity = (cluster_pos, star_vel)
    acceleration, jerk_rate = evaluate(positions, velocity)
    for substep in range(SUBSTEPS):
        guess_pos = positions + substep_time * (
            velocity + substep_time * (acceleration / 2.0 + substep_time * jerk_rate / 6.0)
        )
        guess_vel = velocity + substep_time * (acceleration + substep_time * jerk_rate / 2.0)
        new_acc, new_jerk = evaluate(guess_pos, guess_vel)
        new_vel = (
            velocity
            + substep_time / 2.0 * (acceleration + new_acc)
            + substep_time * substep_time / 12.0 * (jerk_rate - new_jerk)
        )
        new_pos = (
            positions
            + substep_time / 2.0 * (velocity + new_vel)
            + substep_time * substep_time / 12.0 * (acceleration - new_acc)
        )
        positions, velocity, acceleration, jerk_rate = (new_pos, new_vel, new_acc, new_jerk)
    second_pull, second_push = kick(positions, body_pos)
    return (
        positions,
        velocity + half_step * second_pull,
        body_pos,
        body_vel + half_step * second_push,
    )


def solution(mesh):
    return jax.shard_map(
        local,
        mesh=mesh,
        in_specs=(
            P(None, "sub"),
            P(None, "sub"),
            P("sub"),
            P(None, ("grp", "sub")),
            P(None, ("grp", "sub")),
            P(("grp", "sub")),
            P(),
        ),
        out_specs=(
            P(None, "sub"),
            P(None, "sub"),
            P(None, ("grp", "sub")),
            P(None, ("grp", "sub")),
        ),
        check_vma=False,
    )
```

profile of v0, /device:TPU:1, one launch (start us, length us, event | category | flops | bytes accessed | tf_op | source)
XLA Modules:
  0.0 715.4 jit_solution(4176489332510097580)
XLA Ops:
  2.0 40.5 %all_gather.33 = f32[4,4096]{1,0:T(4,128)S(1)} all-gather(f32[4,128]{1,0:T(4,128)S(1)} %pad_maximum_fusion.10), channel_id=1, replica_groups=mesh['grp'=8,'sub'=32] {'sub'}, dimensions={1}, use_global_device_ids=true | all-gather | bytes 67584 | tf_op jit(solution)/shard_map/all_gather | solution.py:79
  43.3 14.5 %while.8 = (s32[]{:T(128)}, f32[4,3,1024]{2,1,0:T(4,128)S(1)}, f32[3,512]{1,0:T(4,128)}, f32[4,3,1024]{2,1,0:T(4,128)S(1)}, f32[512]{0:T(512)S(1)}, /*index=5*/s32[]{:T(128)}) while((s32[]{:T(128)}, f32[4,3,1024]{2,1,0:T(4,128)S(1)}, f32[3,512]{1,0:T(4,128)}, f32[4,3,1024]{2,1,0:T(4,128)S(1)}, f32[512]{0:T(512)S(1)}, ...), condition=%wide.region_4.5_spmd, body=%wide.region_1.4_spmd.sunk | while | flops 11006978 | bytes 8521833 | solution.py:34
  57.8 87.6 %psum.14 = f32[3,4096]{1,0:T(4,128)S(1)} all-reduce(f32[3,4096]{1,0:T(4,128)S(1)} %bitcast.93), channel_id=1, replica_groups=mesh['grp'=8,'sub'=32] {'grp','sub'}, use_global_device_ids=true, to_apply=%region_5.6 | all-reduce | flops 12288 | bytes 98304 | tf_op jit(solution)/shard_map/psum | solution.py:82
  145.4 31.0 %all_gather.34 = f32[7,4096]{1,0:T(8,128)S(1)} all-gather(f32[7,128]{1,0:T(8,128)S(1)} %pad_maximum_fusion.8), channel_id=1, replica_groups=mesh['grp'=8,'sub'=32] {'sub'}, dimensions={1}, use_global_device_ids=true | all-gather | bytes 118272 | tf_op jit(solution)/shard_map/all_gather | solution.py:91
  181.2 32.3 %all_gather.35 = f32[7,4096]{1,0:T(8,128)S(1)} all-gather(f32[7,128]{1,0:T(8,128)S(1)} %pad_maximum_fusion.7), channel_id=1, replica_groups=mesh['grp'=8,'sub'=32] {'sub'}, dimensions={1}, use_global_device_ids=true | all-gather | bytes 118272 | tf_op jit(solution)/shard_map/all_gather | solution.py:91
  216.2 2.2 fusion.11
  218.4 31.8 %all_gather.36 = f32[7,4096]{1,0:T(8,128)S(1)} all-gather(f32[7,128]{1,0:T(8,128)S(1)} %pad_maximum_fusion.6), channel_id=1, replica_groups=mesh['grp'=8,'sub'=32] {'sub'}, dimensions={1}, use_global_device_ids=true | all-gather | bytes 118272 | tf_op jit(solution)/shard_map/all_gather | solution.py:91
  252.9 2.2 fusion.13
  255.1 33.7 %all_gather.37 = f32[7,4096]{1,0:T(8,128)S(1)} all-gather(f32[7,128]{1,0:T(8,128)S(1)} %pad_maximum_fusion.5), channel_id=1, replica_groups=mesh['grp'=8,'sub'=32] {'sub'}, dimensions={1}, use_global_device_ids=true | all-gather | bytes 118272 | tf_op jit(solution)/shard_map/all_gather | solution.py:91
  291.5 2.2 fusion.15
  293.7 30.9 %all_gather.38 = f32[7,4096]{1,0:T(8,128)S(1)} all-gather(f32[7,128]{1,0:T(8,128)S(1)} %pad_maximum_fusion.4), channel_id=1, replica_groups=mesh['grp'=8,'sub'=32] {'sub'}, dimensions={1}, use_global_device_ids=true | all-gather | bytes 118272 | tf_op jit(solution)/shard_map/all_gather | solution.py:91
  327.3 2.2 fusion.17
  329.5 33.5 %all_gather.39 = f32[7,4096]{1,0:T(8,128)S(1)} all-gather(f32[7,128]{1,0:T(8,128)S(1)} %pad_maximum_fusion.3), channel_id=1, replica_groups=mesh['grp'=8,'sub'=32] {'sub'}, dimensions={1}, use_global_device_ids=true | all-gather | bytes 118272 | tf_op jit(solution)/shard_map/all_gather | solution.py:91
  365.7 2.2 fusion.19
  367.9 30.7 %all_gather.40 = f32[7,4096]{1,0:T(8,128)S(1)} all-gather(f32[7,128]{1,0:T(8,128)S(1)} %pad_maximum_fusion.2), channel_id=1, replica_groups=mesh['grp'=8,'sub'=32] {'sub'}, dimensions={1}, use_global_device_ids=true | all-gather | bytes 118272 | tf_op jit(solution)/shard_map/all_gather | solution.py:91
  401.3 2.2 fusion.21
  403.5 33.4 %all_gather.41 = f32[7,4096]{1,0:T(8,128)S(1)} all-gather(f32[7,128]{1,0:T(8,128)S(1)} %pad_maximum_fusion.1), channel_id=1, replica_groups=mesh['grp'=8,'sub'=32] {'sub'}, dimensions={1}, use_global_device_ids=true | all-gather | bytes 118272 | tf_op jit(solution)/shard_map/all_gather | solution.py:91
  439.6 2.2 fusion.23
  441.8 31.1 %all_gather.42 = f32[7,4096]{1,0:T(8,128)S(1)} all-gather(f32[7,128]{1,0:T(8,128)S(1)} %pad_maximum_fusion), channel_id=1, replica_groups=mesh['grp'=8,'sub'=32] {'sub'}, dimensions={1}, use_global_device_ids=true | all-gather | bytes 118272 | tf_op jit(solution)/shard_map/all_gather | solution.py:91
  477.9 36.5 %all_gather.43 = f32[4,4096]{1,0:T(4,128)S(1)} all-gather(f32[4,128]{1,0:T(4,128)S(1)} %pad_maximum_fusion.9), channel_id=1, replica_groups=mesh['grp'=8,'sub'=32] {'sub'}, dimensions={1}, use_global_device_ids=true | all-gather | bytes 67584 | tf_op jit(solution)/shard_map/all_gather | solution.py:79
  514.4 8.5 %while.9 = (s32[]{:T(128)}, f32[4,3,128]{2,1,0:T(4,128)S(1)}, f32[3,4096]{1,0:T(4,128)S(1)}, f32[4,3,128]{2,1,0:T(4,128)S(1)}, f32[1,4096]{1,0:T(1,128)S(1)}, /*index=5*/s32[]{:T(128)}) while((s32[]{:T(128)}, f32[4,3,128]{2,1,0:T(4,128)S(1)}, f32[3,4096]{1,0:T(4,128)S(1)}, f32[4,3,128]{2,1,0:T(4,128)S(1)}, f32[1,4096]{1,0:T(1,128)S(1)}, ...), condition=%wide.region_45.46_spmd, body=%wide.region_42.45_spmd.sunk | while | flops 11009666 | bytes 8515149 | solution.py:34
  523.0 8.5 %while.11 = (s32[]{:T(128)}, f32[4,3,128]{2,1,0:T(4,128)S(1)}, f32[3,4096]{1,0:T(4,128)S(1)}, f32[4,3,128]{2,1,0:T(4,128)S(1)}, f32[1,4096]{1,0:T(1,128)S(1)}, /*index=5*/s32[]{:T(128)}) while((s32[]{:T(128)}, f32[4,3,128]{2,1,0:T(4,128)S(1)}, f32[3,4096]{1,0:T(4,128)S(1)}, f32[4,3,128]{2,1,0:T(4,128)S(1)}, f32[1,4096]{1,0:T(1,128)S(1)}, ...), condition=%wide.region_54.55_spmd, body=%wide.region_51.54_spmd.sunk | while | flops 11009666 | bytes 8515149 | solution.py:34
  532.1 10.4 %while.10 = (s32[]{:T(128)}, f32[4,3,1024]{2,1,0:T(4,128)S(1)}, f32[3,512]{1,0:T(4,128)S(1)}, f32[4,3,1024]{2,1,0:T(4,128)S(1)}, f32[512]{0:T(512)S(1)}, /*index=5*/s32[]{:T(128)}) while((s32[]{:T(128)}, f32[4,3,1024]{2,1,0:T(4,128)S(1)}, f32[3,512]{1,0:T(4,128)S(1)}, f32[4,3,1024]{2,1,0:T(4,128)S(1)}, f32[512]{0:T(512)S(1)}, ...), condition=%wide.region_49.50_spmd, body=%wide.region_46.49_spmd.sunk | while | flops 11006978 | bytes 8497229 | solution.py:34
  542.5 171.9 %psum.15 = f32[3,4096]{1,0:T(4,128)S(1)} all-reduce(f32[3,4096]{1,0:T(4,128)S(1)} %bitcast.92), channel_id=1, replica_groups=mesh['grp'=8,'sub'=32] {'grp','sub'}, use_global_device_ids=true, to_apply=%region_50.51 | all-reduce | flops 12288 | bytes 98304 | tf_op jit(solution)/shard_map/psum | solution.py:82
  (174 shorter events, 72.9 us)
Async XLA Ops:
  43.2 102.1 %copy-start.6 = (f32[3,128]{1,0:T(4,128)S(1)}, f32[3,128]{1,0:T(4,128)}, u32[]{:S(2)}) copy-start(f32[3,128]{1,0:T(4,128)} %param.16) | copy-start | bytes 4612
  43.2 102.1 %copy-start.3 = (f32[3,128]{1,0:T(4,128)S(1)}, f32[3,128]{1,0:T(4,128)}, u32[]{:S(2)}) copy-start(f32[3,128]{1,0:T(4,128)} %param.15) | copy-start | bytes 4612
  44.9 0.7 copy-start
  48.6 0.7 copy-start
  52.2 0.7 copy-start
  55.8 0.7 copy-start
  475.6 38.8 %copy-start.1 = (f32[3,512]{1,0:T(4,128)S(1)}, f32[3,512]{1,0:T(4,128)}, u32[]{:S(2)}) copy-start(f32[3,512]{1,0:T(4,128)} %get-tuple-element.607) | copy-start | bytes 18436
  477.8 36.6 %copy-start.5 = (f32[3,128]{1,0:T(4,128)}, f32[3,128]{1,0:T(4,128)S(1)}, u32[]{:S(2)}) copy-start(f32[3,128]{1,0:T(4,128)S(1)} %multiply_add_fusion.2) | copy-start | bytes 4612
  514.4 8.5 %copy-start.4 = (f32[3,512]{1,0:T(4,128)S(1)}, f32[3,512]{1,0:T(4,128)}, u32[]{:S(2)}) copy-start(f32[3,512]{1,0:T(4,128)} %param.19) | copy-start | bytes 18436
  542.5 172.5 %copy-start.2 = (f32[3,512]{1,0:T(4,128)}, f32[3,512]{1,0:T(4,128)S(1)}, u32[]{:S(2)}) copy-start(f32[3,512]{1,0:T(4,128)S(1)} %get-tuple-element.610) | copy-start | bytes 18436
where the time goes:
time: 725 us; the launch traced here: 715 us
  blocking collectives  625 us (86%)
  other arithmetic  86 us (12%)
    all_gather x9, blocking collectives, evaluate(): source_piece = lax.all_gather(sources, 'sub', axis=1, tiled=True)  288 us
    psum x2, blocking collectives, kick(): summed = lax.psum(partial_value, ('grp', 'sub'))  259 us
    all_gather x2, blocking collectives, kick(): gathered = lax.all_gather(stacked, 'sub', axis=1, tiled=True)  76.9 us
    reduce_sum x8, other arithmetic, rates_one_tile(): jnp.sum((closing - radial[None] * separation) * weight[None], axis=2)  17.5 us
    reduce_sum x16, other arithmetic, field_one_tile(): distance = jnp.sum(separation * separation, axis=0) + soften  17.3 us
    reduce_sum x16, other arithmetic, field_one_tile(): return jnp.sum(separation * weight[None], axis=2)  16.5 us
    reduce_sum x8, other arithmetic, rates_one_tile(): radial = 3.0 * jnp.sum(separation * closing, axis=0) / distance  16.4 us

commit v1 on v0

--- a/solution.py
+++ b/solution.py
@@ -79,7 +79,7 @@
         gathered = lax.all_gather(stacked, "sub", axis=1, tiled=True)
         galaxy_push = field(body_positions, gathered[:3], gathered[3], bridge_soft)
         partial_value = field(gathered[:3], body_positions, body_mass, bridge_soft)
-        summed = lax.psum(partial_value, ("grp", "sub"))
+        summed = jnp.sum(lax.all_gather(partial_value, ("grp", "sub")), axis=0)
         cluster_pull = lax.dynamic_slice_in_dim(
             summed, lax.axis_index("sub") * star_count, star_count, 1
         )

time: 725 us -> 836 us (1.15)
  waiting for transfers between devices: 0 us -> 336 us
  blocking collectives: 625 us -> 366 us
  other arithmetic: 86 us -> 104 us
  between operations: 1.67 us -> 15.1 us
    all_gather x0 -> x2, waiting for transfers between devices: none -> 336 us  [kick(): summed = jnp.sum(lax.all_gather(partial_value, ('grp', 'sub')), axis=0)]
    psum x2 -> x0, blocking collectives: 259 us -> none  [kick(): summed = lax.psum(partial_value, ('grp', 'sub'))]
    reduce_sum x0 -> x2, other arithmetic: none -> 17.6 us  [kick(): summed = jnp.sum(lax.all_gather(partial_value, ('grp', 'sub')), axis=0)]
  transfers between devices with their start and end apart: 0 -> 2, of which waited for: 0 -> 2; matrix products, arithmetic and copies ran while one was open for 0% -> 3% of each run, Pallas kernels for 0% -> 0%
where the time goes in v1:
time: 836 us; the launch traced here: 829 us
  blocking collectives  366 us (44%)
  waiting for transfers between devices  336 us (40%)
  other arithmetic  104 us (12%)
  between operations  15.1 us (2%)
    all_gather x2, waiting for transfers between devices, kick(): summed = jnp.sum(lax.all_gather(partial_value, ('grp', 'sub')), axis=0)  336 us
    all_gather x9, blocking collectives, evaluate(): source_piece = lax.all_gather(sources, 'sub', axis=1, tiled=True)  291 us
    all_gather x2, blocking collectives, kick(): gathered = lax.all_gather(stacked, 'sub', axis=1, tiled=True)  75.7 us
    reduce_sum x2, other arithmetic, kick(): summed = jnp.sum(lax.all_gather(partial_value, ('grp', 'sub')), axis=0)  17.6 us
    reduce_sum x8, other arithmetic, rates_one_tile(): jnp.sum((closing - radial[None] * separation) * weight[None], axis=2)  17.5 us
    reduce_sum x16, other arithmetic, field_one_tile(): distance = jnp.sum(separation * separation, axis=0) + soften  17.3 us
  transfers between devices with their start and end apart: 2, of which 2 were waited for; matrix products, arithmetic and copies ran while one was open for 3% of the time, Pallas kernels for 0%

profile of v1, /device:TPU:1, one launch (start us, length us, event | category | flops | bytes accessed | tf_op | source)
XLA Modules:
  0.0 828.5 jit_solution(17297801181655927765)
XLA Ops:
  8.6 40.5 %all_gather.39 = f32[4,4096]{1,0:T(4,128)S(1)} all-gather(f32[4,128]{1,0:T(4,128)S(1)} %pad_maximum_fusion.10), channel_id=1, replica_groups=mesh['grp'=8,'sub'=32] {'sub'}, dimensions={1}, use_global_device_ids=true | all-gather | bytes 67584 | tf_op jit(solution)/shard_map/all_gather | solution.py:79
  49.8 14.5 %while.8 = (s32[]{:T(128)}, f32[4,3,1024]{2,1,0:T(4,128)S(1)}, f32[3,512]{1,0:T(4,128)}, f32[4,3,1024]{2,1,0:T(4,128)S(1)}, f32[512]{0:T(512)S(1)}, /*index=5*/s32[]{:T(128)}) while((s32[]{:T(128)}, f32[4,3,1024]{2,1,0:T(4,128)S(1)}, f32[3,512]{1,0:T(4,128)}, f32[4,3,1024]{2,1,0:T(4,128)S(1)}, f32[512]{0:T(512)S(1)}, ...), condition=%wide.region_4.5_spmd, body=%wide.region_1.4_spmd.sunk | while | flops 11006978 | bytes 8521833 | solution.py:34
  65.1 11.2 %while.9 = (s32[]{:T(128)}, f32[4,3,128]{2,1,0:T(4,128)S(1)}, f32[3,4096]{1,0:T(4,128)S(1)}, f32[4,3,128]{2,1,0:T(4,128)}, f32[1,4096]{1,0:T(1,128)S(1)}, /*index=5*/s32[]{:T(128)}) while((s32[]{:T(128)}, f32[4,3,128]{2,1,0:T(4,128)S(1)}, f32[3,4096]{1,0:T(4,128)S(1)}, f32[4,3,128]{2,1,0:T(4,128)}, f32[1,4096]{1,0:T(1,128)S(1)}, ...), condition=%wide.region_45.46_spmd, body=%wide.region_42.45_spmd.sunk | while | flops 11009666 | bytes 8515149 | solution.py:34
  77.0 124.1 %all-gather.3.cloned.1.call-done = f32[256,3,4096]{2,1,0:T(4,128)} async-done(((f32[1,3,4096]{2,1,0:T(4,128)}), f32[256,3,4096]{2,1,0:T(4,128)}) %all-gather.3.cloned.1.call-update) | async-done | bytes 12582928 | tf_op jit(solution)/shard_map/all_gather | solution.py:82
  201.0 8.8 %reduce_sum.460 = f32[3,4096]{1,0:T(4,128)S(1)} reduce(f32[256,3,4096]{2,1,0:T(4,128)} %all-gather.3.cloned.1.call-done, f32[]{:T(128)} %constant.221.clone.1), dimensions={0}, to_apply=%region_5.6 | reduce | flops 3133440 | bytes 12632068 | tf_op jit(solution)/shard_map/reduce_sum | solution.py:82
  209.9 33.2 %all_gather.41 = f32[7,4096]{1,0:T(8,128)S(1)} all-gather(f32[7,128]{1,0:T(8,128)S(1)} %pad_maximum_fusion.8), channel_id=1, replica_groups=mesh['grp'=8,'sub'=32] {'sub'}, dimensions={1}, use_global_device_ids=true | all-gather | bytes 118272 | tf_op jit(solution)/shard_map/all_gather | solution.py:91
  247.8 31.9 %all_gather.42 = f32[7,4096]{1,0:T(8,128)S(1)} all-gather(f32[7,128]{1,0:T(8,128)S(1)} %pad_maximum_fusion.7), channel_id=1, replica_groups=mesh['grp'=8,'sub'=32] {'sub'}, dimensions={1}, use_global_device_ids=true | all-gather | bytes 118272 | tf_op jit(solution)/shard_map/all_gather | solution.py:91
  282.4 2.2 fusion.11
  284.7 32.7 %all_gather.43 = f32[7,4096]{1,0:T(8,128)S(1)} all-gather(f32[7,128]{1,0:T(8,128)S(1)} %pad_maximum_fusion.6), channel_id=1, replica_groups=mesh['grp'=8,'sub'=32] {'sub'}, dimensions={1}, use_global_device_ids=true | all-gather | bytes 118272 | tf_op jit(solution)/shard_map/all_gather | solution.py:91
  320.0 2.2 fusion.13
  322.3 32.2 %all_gather.44 = f32[7,4096]{1,0:T(8,128)S(1)} all-gather(f32[7,128]{1,0:T(8,128)S(1)} %pad_maximum_fusion.5), channel_id=1, replica_groups=mesh['grp'=8,'sub'=32] {'sub'}, dimensions={1}, use_global_device_ids=true | all-gather | bytes 118272 | tf_op jit(solution)/shard_map/all_gather | solution.py:91
  357.1 2.2 fusion.15
  359.4 32.6 %all_gather.45 = f32[7,4096]{1,0:T(8,128)S(1)} all-gather(f32[7,128]{1,0:T(8,128)S(1)} %pad_maximum_fusion.4), channel_id=1, replica_groups=mesh['grp'=8,'sub'=32] {'sub'}, dimensions={1}, use_global_device_ids=true | all-gather | bytes 118272 | tf_op jit(solution)/shard_map/all_gather | solution.py:91
  394.7 2.2 fusion.17
  396.9 31.6 %all_gather.46 = f32[7,4096]{1,0:T(8,128)S(1)} all-gather(f32[7,128]{1,0:T(8,128)S(1)} %pad_maximum_fusion.3), channel_id=1, replica_groups=mesh['grp'=8,'sub'=32] {'sub'}, dimensions={1}, use_global_device_ids=true | all-gather | bytes 118272 | tf_op jit(solution)/shard_map/all_gather | solution.py:91
  431.2 2.2 fusion.19
  433.4 31.9 %all_gather.47 = f32[7,4096]{1,0:T(8,128)S(1)} all-gather(f32[7,128]{1,0:T(8,128)S(1)} %pad_maximum_fusion.2), channel_id=1, replica_groups=mesh['grp'=8,'sub'=32] {'sub'}, dimensions={1}, use_global_device_ids=true | all-gather | bytes 118272 | tf_op jit(solution)/shard_map/all_gather | solution.py:91
  470.2 32.1 %all_gather.48 = f32[7,4096]{1,0:T(8,128)S(1)} all-gather(f32[7,128]{1,0:T(8,128)S(1)} %pad_maximum_fusion.1), channel_id=1, replica_groups=mesh['grp'=8,'sub'=32] {'sub'}, dimensions={1}, use_global_device_ids=true | all-gather | bytes 118272 | tf_op jit(solution)/shard_map/all_gather | solution.py:91
  507.2 32.5 %all_gather.49 = f32[7,4096]{1,0:T(8,128)S(1)} all-gather(f32[7,128]{1,0:T(8,128)S(1)} %pad_maximum_fusion), channel_id=1, replica_groups=mesh['grp'=8,'sub'=32] {'sub'}, dimensions={1}, use_global_device_ids=true | all-gather | bytes 118272 | tf_op jit(solution)/shard_map/all_gather | solution.py:91
  544.6 35.3 %all_gather.50 = f32[4,4096]{1,0:T(4,128)S(1)} all-gather(f32[4,128]{1,0:T(4,128)S(1)} %pad_maximum_fusion.9), channel_id=1, replica_groups=mesh['grp'=8,'sub'=32] {'sub'}, dimensions={1}, use_global_device_ids=true | all-gather | bytes 67584 | tf_op jit(solution)/shard_map/all_gather | solution.py:79
  579.9 10.4 %while.10 = (s32[]{:T(128)}, f32[4,3,1024]{2,1,0:T(4,128)S(1)}, f32[3,512]{1,0:T(4,128)S(1)}, f32[4,3,1024]{2,1,0:T(4,128)S(1)}, f32[512]{0:T(512)S(1)}, /*index=5*/s32[]{:T(128)}) while((s32[]{:T(128)}, f32[4,3,1024]{2,1,0:T(4,128)S(1)}, f32[3,512]{1,0:T(4,128)S(1)}, f32[4,3,1024]{2,1,0:T(4,128)S(1)}, f32[512]{0:T(512)S(1)}, ...), condition=%wide.region_49.50_spmd, body=%wide.region_46.49_spmd.sunk | while | flops 11006978 | bytes 8497229 | solution.py:34
  591.0 8.5 %while.11 = (s32[]{:T(128)}, f32[4,3,128]{2,1,0:T(4,128)S(1)}, f32[3,4096]{1,0:T(4,128)S(1)}, f32[4,3,128]{2,1,0:T(4,128)S(1)}, f32[1,4096]{1,0:T(1,128)S(1)}, /*index=5*/s32[]{:T(128)}) while((s32[]{:T(128)}, f32[4,3,128]{2,1,0:T(4,128)S(1)}, f32[3,4096]{1,0:T(4,128)S(1)}, f32[4,3,128]{2,1,0:T(4,128)S(1)}, f32[1,4096]{1,0:T(1,128)S(1)}, ...), condition=%wide.region_54.55_spmd, body=%wide.region_51.54_spmd.sunk | while | flops 11009666 | bytes 8515149 | solution.py:34
  600.1 211.7 %all-gather.5.cloned.1.call-done = f32[256,3,4096]{2,1,0:T(4,128)} async-done(((f32[1,3,4096]{2,1,0:T(4,128)}), f32[256,3,4096]{2,1,0:T(4,128)}) %all-gather.5.cloned.1.call-update) | async-done | bytes 12582928 | tf_op jit(solution)/shard_map/all_gather | solution.py:82
  811.8 8.8 %reduce_sum.497 = f32[3,4096]{1,0:T(4,128)S(1)} reduce(f32[256,3,4096]{2,1,0:T(4,128)} %all-gather.5.cloned.1.call-done, f32[]{:T(128)} %constant.221.clone.1), dimensions={0}, to_apply=%region_50.51 | reduce | flops 3133440 | bytes 12632068 | tf_op jit(solution)/shard_map/reduce_sum | solution.py:82
  (182 shorter events, 82.0 us)
Async XLA Ops:
  7.2 193.9 %all-gather.3.cloned.1.call-start = ((), (), s32[]{:S(2)}) async-start(), calls=%async_computation | async-start | bytes 16842752 | tf_op jit(solution)/shard_map/all_gather | solution.py:82
  51.5 0.7 copy-start
  55.1 0.7 copy-start
  58.7 0.7 copy-start
  62.4 0.7 copy-start
  64.3 0.6 copy-start.2
  65.0 746.8 %all-gather.5.cloned.1.call-start = ((), (), s32[]{:S(2)}) async-start(), calls=%async_computation.1 | async-start | bytes 16842752 | tf_op jit(solution)/shard_map/all_gather | solution.py:82
  65.1 11.2 %copy-start.5 = (f32[3,512]{1,0:T(4,128)S(1)}, f32[3,512]{1,0:T(4,128)}, u32[]{:S(2)}) copy-start(f32[3,512]{1,0:T(4,128)} %param.19) | copy-start | bytes 18436
  77.0 132.9 %copy-start.7 = (f32[3,128]{1,0:T(4,128)S(1)}, f32[3,128]{1,0:T(4,128)}, u32[]{:S(2)}) copy-start(f32[3,128]{1,0:T(4,128)} %param.16) | copy-start | bytes 4612
  77.0 132.9 %copy-start.4 = (f32[3,128]{1,0:T(4,128)S(1)}, f32[3,128]{1,0:T(4,128)}, u32[]{:S(2)}) copy-start(f32[3,128]{1,0:T(4,128)} %param.15) | copy-start | bytes 4612
  544.6 35.3 %copy-start.6 = (f32[3,128]{1,0:T(4,128)}, f32[3,128]{1,0:T(4,128)S(1)}, u32[]{:S(2)}) copy-start(f32[3,128]{1,0:T(4,128)S(1)} %multiply_add_fusion.2) | copy-start | bytes 4612
  590.3 0.6 copy-start.3
  599.5 221.1 %copy-start.1 = (f32[4,3,128]{2,1,0:T(4,128)}, f32[4,3,128]{2,1,0:T(4,128)S(1)}, u32[]{:S(2)}) copy-start(f32[4,3,128]{2,1,0:T(4,128)S(1)} %get-tuple-element.614) | copy-start | bytes 18436
Sparse Core Ops, SparseCore 0:
  65.1 135.9 all-gather.2
  591.1 220.6 all-gather.4
